TPU v7x, 32 devices: a whole 2x2x4 slice. The times are simulated.
32 devices in a mesh: tile: 8 (over z, y), clip: 4 (over x, core).
Axes of the slice: x: 2, y: 2, z: 4, core: 2. Of those that a mesh axis runs over, the one named last changes fastest.
Arguments:
- seq_rows: bfloat16 [32768, 512], P(('tile', 'clip'))
- plan_owner: int32 [32768], P(('tile', 'clip')), may hold values from 0 to 31, as said below
- plan_slot: int32 [32768], P(('tile', 'clip')), may hold values from 0 to 1023, as said below
- live_frames: int32 [4], replicated, may hold values from 1 to 4, as said below
- norm_gain: float32 [512], replicated, may hold values from 0.1 to 1.9
- norm_bias: float32 [512], replicated, may hold values from -3 to 3
- conv_weight: bfloat16 [3, 3, 512, 3, 256], replicated, may hold values from -0.0546875 to 0.0546875
- conv_bias: float32 [256], replicated, may hold values from -3 to 3
Outputs:
- decoded: bfloat16 [4, 8, 4, 8, 32, 256], P('clip', 'tile')
Inputs may be any that keep to these rules, and one draw needn't show every extreme that they name: `plan_owner`: owner o is tile o % 8 of clip o // 8. The 1024 rows of each device send 32 // 2 or 48 rows to each owner, so at most 48, which is reached. The pairs of plan_owner and plan_slot are all distinct: every slot of every owner receives exactly one row. `live_frames`: some clip has all 4 frames live.
All inputs are finite; a program needn't handle non-finite values.
Results may differ from a plain program's by a relative error of at most 0.004.
Values may be sent and summed in bfloat16 or wider, within the bound.
A program may use at most 128 MiB of HBM per device.

v0:
```python
import jax
import jax.numpy as jnp
from jax import lax
from jax.sharding import PartitionSpec as P

GROUPS = 32
LT = 4
TH = 8
TW = 32
GW = 4


EPSILON = 1e-06
HIGHEST = lax.Precision.HIGHEST


def shifted(block, axis, distance):
    devices = range(lax.axis_size(axis))
    route = [(i - distance, i) for i in devices if i - distance in devices]
    return lax.ppermute(block, axis, route)


def neighbour(values, offset):
    return shifted(values, "tile", offset)


def extend(tile_grid, column_tile, grid_cols):
    left_face = neighbour(tile_grid[:, :, -1:], 1)
    right_face = neighbour(tile_grid[:, :, :1], -1)
    left_face = jnp.where(column_tile > 0, left_face, jnp.zeros_like(left_face))
    right_face = jnp.where(column_tile < grid_cols - 1, right_face, jnp.zeros_like(right_face))
    widened = jnp.concatenate([left_face, tile_grid, right_face], axis=2)
    upper_face = neighbour(widened[:, -1:], grid_cols)
    lower_face = neighbour(widened[:, :1], -grid_cols)
    return jnp.concatenate([upper_face, widened, lower_face], axis=1)


def normalize(values, mean_channel, scale_channel, norm_gain, norm_bias):
    normed = (values.astype(jnp.float32) - mean_channel) * scale_channel * norm_gain + norm_bias
    return jax.nn.silu(normed)


def on_device(
    seq_rows, plan_owner, plan_slot, live_frames, norm_gain, norm_bias, conv_weight, conv_bias
):
    row_count, channels = seq_rows.shape
    out_width = conv_bias.shape[0]
    tile_count = lax.axis_size("tile")
    clip_count = lax.axis_size("clip")
    owner_count = tile_count * clip_count
    capacity = 3 * (row_count // owner_count) // 2
    per_group = channels // GROUPS
    plane_size = TH * TW
    voxel_total = float(plane_size * tile_count)
    row_index = jnp.arange(row_count, dtype=jnp.int32)
    owner_table = (plan_owner[:, None] == jnp.arange(owner_count, dtype=jnp.int32)[None, :]).astype(
        jnp.int32
    )
    ranking = jnp.sum((jnp.cumsum(owner_table, axis=0) - 1) * owner_table, axis=1)
    position = plan_owner * capacity + ranking
    my_clip = lax.axis_index("clip")
    my_tile = lax.axis_index("tile")
    frames_live = live_frames[my_clip]
    outgoing = (
        jnp.zeros((owner_count * capacity, channels), jnp.bfloat16).at[position].set(seq_rows)
    )
    slot_list = (
        jnp.full((owner_count * capacity,), row_count, jnp.int32).at[position].set(plan_slot)
    )
    outgoing = outgoing.reshape(clip_count, tile_count, capacity, channels)
    slot_list = slot_list.reshape(clip_count, tile_count, capacity)
    arrived, arrived_slots = (
        lax.all_to_all(
            lax.all_to_all(outgoing, "tile", split_axis=1, concat_axis=1, tiled=True),
            "clip",
            split_axis=0,
            concat_axis=0,
            tiled=True,
        ),
        lax.all_to_all(
            lax.all_to_all(slot_list, "tile", split_axis=1, concat_axis=1, tiled=True),
            "clip",
            split_axis=0,
            concat_axis=0,
            tiled=True,
        ),
    )
    tile_rows = (
        jnp.zeros((row_count, channels), jnp.bfloat16)
        .at[arrived_slots.reshape(-1)]
        .set(arrived.reshape(-1, channels), mode="drop")
    )
    grid_cols = GW
    grid_rows = tile_count // grid_cols
    column_tile = my_tile % grid_cols
    row_tile = my_tile // grid_cols
    live_frame = jnp.arange(LT) < frames_live
    values = tile_rows.astype(jnp.float32)
    live_row = (row_index // plane_size < frames_live).astype(jnp.float32)
    first_sum = jnp.dot(live_row, values, precision=HIGHEST).reshape(GROUPS, per_group).sum(axis=1)
    second_sum = (
        jnp.dot(live_row, values * values, precision=HIGHEST).reshape(GROUPS, per_group).sum(axis=1)
    )
    raw_padded = extend(tile_rows.reshape(LT, TH, TW, channels), column_tile, grid_cols)
    first_sum, second_sum = lax.psum((first_sum, second_sum), "tile")
    count_clip = per_group * frames_live.astype(jnp.float32) * voxel_total
    mean_group = first_sum / count_clip
    scale_group = lax.rsqrt(second_sum / count_clip - mean_group * mean_group + EPSILON)
    mean_channel = jnp.repeat(mean_group, per_group)
    scale_channel = jnp.repeat(scale_group, per_group)
    inside_rows = jnp.arange(TH + 2)
    inside_cols = jnp.arange(TW + 2)
    rows_inside = ((inside_rows > 0) | (row_tile > 0)) & (
        (inside_rows < TH + 1) | (row_tile < grid_rows - 1)
    )
    cols_inside = ((inside_cols > 0) | (column_tile > 0)) & (
        (inside_cols < TW + 1) | (column_tile < grid_cols - 1)
    )
    valid_mask = rows_inside[:, None] & cols_inside[None, :]
    activated = normalize(raw_padded, mean_channel, scale_channel, norm_gain, norm_bias)
    padded = jnp.where(valid_mask[None, :, :, None], activated, 0.0).astype(jnp.bfloat16)
    padded = jnp.concatenate(
        [jnp.zeros((2, TH + 2, TW + 2, channels), jnp.bfloat16), padded], axis=0
    )
    accumulated = jnp.zeros((LT, TH, TW, out_width), jnp.float32)
    for tap_t in range(3):
        for tap_h in range(3):
            slab_rows = padded[tap_t : tap_t + LT, tap_h : tap_h + TH].reshape(-1, channels)
            kernel = conv_weight[tap_t, tap_h].reshape(channels, 3 * out_width)
            product = jnp.dot(slab_rows, kernel, preferred_element_type=jnp.float32)
            product = product.reshape(LT, TH, TW + 2, 3, out_width)
            for tap_w in range(3):
                accumulated = accumulated + product[:, :, tap_w : tap_w + TW, tap_w]
    decoded = jnp.where(live_frame[:, None, None, None], accumulated + conv_bias, 0.0)
    return decoded.astype(jnp.bfloat16)[None, None]


def solution(mesh):
    return jax.shard_map(
        on_device,
        mesh=mesh,
        in_specs=(
            P(("tile", "clip"), None),
            P(("tile", "clip")),
            P(("tile", "clip")),
            P(),
            P(),
            P(),
            P(),
            P(),
        ),
        out_specs=P("clip", "tile", None, None, None, None),
        check_vma=False,
    )
```

profile of v0, /device:TPU:0, one launch (start us, length us, event | category | flops | bytes accessed | tf_op | source)
XLA Modules:
  0.0 185.9 jit_solution(9642833911319196824)
XLA Ops:
  0.0 0.7 fusion.53
  0.7 9.0 %reduce-window.6 = s32[32,8,128]{2,1,0:T(8,128)S(1)} reduce-window(s32[32,8,128]{2,1,0:T(8,128)S(1)} %fusion.53, s32[]{:T(128)} %constant.69.clone.1), window={size=1x1x128 pad=0_0x0_0x127_0}, to_apply=%region_0.0 | reduce-window | flops 4161536 | bytes 262148 | tf_op jit(solution)/shard_map/reduce-window
  10.2 0.7 fusion.52
  10.9 0.7 compare_select_fusion.1
  11.6 4.5 %scatter_custom_fusion = s32[1536]{0:T(1024)S(1)} fusion(s32[1024]{0:T(1024)S(1)} %compare_select_fusion.1, s32[1024]{0:T(1024)} %param.10, s32[]{:T(128)} %constant.80.clone.1), kind=kCustom, calls=%fused_computation.106 | custom fusion | bytes 6656 | tf_op jit(solution)/shard_map/scatter | solution.py:68
  16.2 0.7 reshape.525
  16.9 7.3 %all-to-all-start = ((s32[8,1,192]{2,1,0:T(1,128)}), s32[8,1,192]{2,1,0:T(1,128)S(1)}, u32[]{:S(2)}, u32[]{:S(2)}) async-start(s32[8,1,192]{2,1,0:T(1,128)} %reshape.525), calls=%async_computation | async-start | bytes 16384 | tf_op jit(solution)/shard_map/all_to_all | solution.py:81
  24.1 6.0 %scatter_custom_fusion.1 = bf16[1536,512]{1,0:T(8,128)(2,1)S(1)} fusion(s32[1024]{0:T(1024)S(1)} %compare_select_fusion.1, bf16[1024,512]{1,0:T(8,128)(2,1)} %param.8, bf16[]{:T(256)} %constant.79.clone.1), kind=kCustom, calls=%fused_computation.80 | custom fusion | bytes 1573376 | tf_op jit(solution)/shard_map/scatter | solution.py:65
  30.2 1.3 copy.91
  31.5 6.0 %all-to-all-start.2 = ((bf16[4,8,48,512]{3,2,0,1:T(8,128)(2,1)}), bf16[4,8,48,512]{3,2,0,1:T(8,128)(2,1)S(1)}, u32[]{:S(2)}, u32[]{:S(2)}) async-start(bf16[4,8,48,512]{3,2,0,1:T(8,128)(2,1)} %copy.91), calls=%async_computation.2 | async-start | bytes 3145728 | tf_op jit(solution)/shard_map/all_to_all | solution.py:74
  38.0 0.6 reduce.2
  38.8 0.7 reshape.527
  39.4 34.5 %all-to-all-done.2 = bf16[4,8,48,512]{3,2,0,1:T(8,128)(2,1)S(1)} async-done(((bf16[4,8,48,512]{3,2,0,1:T(8,128)(2,1)}), bf16[4,8,48,512]{3,2,0,1:T(8,128)(2,1)S(1)}, u32[]{:S(2)}, u32[]{:S(2)}) %all-to-all-start.2) | async-done | bytes 1572896 | tf_op jit(solution)/shard_map/all_to_all | solution.py:74
  73.9 3.2 %all-to-all-start.1 = ((s32[4,1,384]{2,1,0:T(1,128)}), s32[4,1,384]{2,1,0:T(1,128)S(1)}, u32[]{:S(2)}, u32[]{:S(2)}) async-start(s32[4,1,384]{2,1,0:T(1,128)} %reshape.527), calls=%async_computation.1 | async-start | bytes 12288 | tf_op jit(solution)/shard_map/all_to_all | solution.py:80
  78.4 1.3 copy.92
  79.7 1.3 all-to-all-done.1
  81.0 4.3 %all-to-all-start.3 = ((bf16[4,8,48,512]{3,2,1,0:T(8,128)(2,1)}), bf16[4,8,48,512]{3,2,1,0:T(8,128)(2,1)}, u32[]{:S(2)}, u32[]{:S(2)}) async-start(bf16[4,8,48,512]{3,2,1,0:T(8,128)(2,1)} %copy.92), calls=%async_computation.3 | async-start | bytes 3145728 | tf_op jit(solution)/shard_map/all_to_all | solution.py:73
  85.9 5.5 %fusion.67 = (bf16[1,1,512,3,256]{4,2,3,1,0:T(8,128)(2,1)}, bf16[1,1,512,3,256]{4,2,3,1,0:T(8,128)(2,1)}, bf16[1,1,512,3,256]{4,2,3,1,0:T(8,128)(2,1)}, bf16[1,1...) fusion(bf16[3,3,512,3,256]{4,2,3,1,0:T(8,128)(2,1)} %param.14), kind=kLoop, calls=%fused_computation.122 | loop fusion | bytes 14155776 | tf_op jit(solution)/shard_map/slice | solution.py:129
  91.4 1.4 copy.130
  92.8 2.4 %copy.138 = bf16[1,1,512,3,256]{2,4,3,1,0:T(8,128)(2,1)} copy(bf16[1,1,512,3,256]{4,2,3,1,0:T(8,128)(2,1)} %get-tuple-element.10) | data formatting | bytes 1572864
  95.1 2.3 %copy.137 = bf16[1,1,512,3,256]{2,4,3,1,0:T(8,128)(2,1)} copy(bf16[1,1,512,3,256]{4,2,3,1,0:T(8,128)(2,1)} %get-tuple-element.11) | data formatting | bytes 1572864
  97.4 2.3 %copy.135 = bf16[1,1,512,3,256]{2,4,3,1,0:T(8,128)(2,1)} copy(bf16[1,1,512,3,256]{4,2,3,1,0:T(8,128)(2,1)} %get-tuple-element.12) | data formatting | bytes 1572864
  99.7 1.2 copy.134
  100.9 1.4 copy.133
  102.3 2.3 %copy.132 = bf16[1,1,512,3,256]{2,4,3,1,0:T(8,128)(2,1)} copy(bf16[1,1,512,3,256]{4,2,3,1,0:T(8,128)(2,1)} %get-tuple-element.15) | data formatting | bytes 1572864
  104.6 2.3 %copy.131 = bf16[1,1,512,3,256]{2,4,3,1,0:T(8,128)(2,1)} copy(bf16[1,1,512,3,256]{4,2,3,1,0:T(8,128)(2,1)} %get-tuple-element.16) | data formatting | bytes 1572864
  106.9 1.2 copy.139
  108.8 0.6 reduce.3
  109.7 8.0 %scatter_custom_fusion.2 = bf16[1024,512]{1,0:T(8,128)(2,1)S(1)} fusion(s32[1536]{0:T(1024)S(1)} %fusion.54, bf16[1536,512]{1,0:T(8,128)(2,1)} %bitcast.5, bf16[]{:T(256)} %constant.79.clone.1), kind=kCustom, calls=%fused_computation.82 | custom fusion | bytes 1049088 | tf_op jit(solution)/shard_map/scatter | solution.py:91
  117.7 0.9 fusion
  118.7 3.3 %collective-permute-start = (bf16[4,8,1,512]{3,2,1,0:T(2,128)(2,1)S(1)}, bf16[4,8,1,512]{3,2,1,0:T(2,128)(2,1)S(1)}, u32[]{:S(2)}, u32[]{:S(2)}) collective-permute-start(bf16[4,8,1,512]{3,2,1,0:T(2,128)(2,1)S(1)} %get-tuple-element.20), channel_id=1, source_target_pairs={{0,4},{4,8},{8,12},{12,16},{16,20},{20,24},{24,28},{1,5},{5,9},{9,... | collective-permute-start | bytes 98312 | tf_op jit(solution)/shard_map/ppermute | solution.py:20
  122.7 1.3 collective-permute-start.1
  124.0 20.7 %all-reduce.1 = (f32[32]{0:T(128)S(1)}, f32[32]{0:T(128)S(1)}) all-reduce(f32[32]{0:T(128)S(1)} %reduce_sum.28, f32[32]{0:T(128)S(1)} %reduce_sum.29), channel_id=1, replica_groups=mesh['tile'=8,'clip'=4] {'tile'}, use_global_device_ids=true, to_apply=%region_7.8 | all-reduce | flops 64 | bytes 512 | tf_op jit(solution)/shard_map/psum | solution.py:105
  145.0 1.3 collective-permute-start.2
  146.3 1.3 collective-permute-start.3
  147.9 1.2 collective-permute-done.2
  149.1 6.4 %collective-permute-done.3 = bf16[4,1,34,512]{3,2,1,0:T(8,128)(2,1)S(1)} collective-permute-done((bf16[4,1,34,512]{3,2,1,0:T(8,128)(2,1)S(1)}, bf16[4,1,34,512]{3,2,1,0:T(8,128)(2,1)S(1)}, u32[]{:S(2)}, u32[]{:S(2)}) %collective-permute-start.3) | collective-permute-done | bytes 139296 | tf_op jit(solution)/shard_map/ppermute | solution.py:20
  155.5 2.5 %select_convert_fusion = bf16[4,10,34,512]{3,2,1,0:T(8,128)(2,1)S(1)} fusion(bf16[4,1,34,512]{3,2,1,0:T(8,128)(2,1)S(1)} %collective-permute-done.3, bf16[4,8,1,512]{3,2,1,0:T(2,128)(2,1)S(1)} %broadcast_select_fusion, bf16[4,8,32,512]{3,2,1,0:T(8,128)(2,1)S(1)} %bitcast.241, bf16[4,8,1,512]{3,2,1,0:T(2,128)(2,1)S(1)} %broadcast_select_fusion.1, ...), kind=kLoop, calls=%fused_computation.3 | loop fusion | flops 13926400 | bytes 2793812 | tf_op jit(solution)/shard_map/convert_element_type | solution.py:121
  158.0 2.5 %fusion.21 = f32[4,8,34,3,256]{4,2,1,0,3:T(8,128)S(1)} fusion(bf16[4,10,34,512]{3,2,1,0:T(8,128)(2,1)S(1)} %select_convert_fusion, bf16[1,1,512,3,256]{2,4,3,1,0:T(8,128)(2,1)} %copy.139), kind=kOutput, calls=%fused_computation.26 | convolution fusion | flops 855638016 | bytes 5439488 | tf_op jit(solution)/shard_map/dot_general | solution.py:130
  160.5 1.2 fusion.7
  161.8 1.2 fusion.10
  163.1 1.2 fusion.13
  164.3 1.2 fusion.16
  165.6 3.1 %fusion.19 = f32[4,8,34,3,256]{4,2,3,1,0:T(8,128)} fusion(bf16[4,10,34,512]{3,2,1,0:T(8,128)(2,1)S(1)} %select_convert_fusion, bf16[1,1,512,3,256]{2,4,3,1,0:T(8,128)(2,1)S(1)} %copy-done), kind=kOutput, calls=%fused_computation.24 | convolution fusion | flops 855638016 | bytes 5521408 | tf_op jit(solution)/shard_map/dot_general | solution.py:130
  168.7 3.2 %fusion.23 = f32[4,8,34,3,256]{4,2,1,0,3:T(8,128)} fusion(bf16[4,10,34,512]{3,2,1,0:T(8,128)(2,1)S(1)} %select_convert_fusion, bf16[1,1,512,3,256]{2,4,3,1,0:T(8,128)(2,1)S(1)} %copy-done.5), kind=kOutput, calls=%fused_computation.30 | convolution fusion | flops 855638016 | bytes 5439488 | tf_op jit(solution)/shard_map/dot_general | solution.py:130
  171.9 3.2 %fusion.22 = f32[4,8,34,3,256]{4,2,1,0,3:T(8,128)} fusion(bf16[4,10,34,512]{3,2,1,0:T(8,128)(2,1)S(1)} %select_convert_fusion, bf16[1,1,512,3,256]{2,4,3,1,0:T(8,128)(2,1)S(1)} %copy-done.4), kind=kOutput, calls=%fused_computation.28 | convolution fusion | flops 855638016 | bytes 5439488 | tf_op jit(solution)/shard_map/dot_general | solution.py:130
  175.1 3.2 %fusion.4 = f32[4,8,34,3,256]{4,2,3,1,0:T(8,128)} fusion(bf16[4,10,34,512]{3,2,1,0:T(8,128)(2,1)S(1)} %select_convert_fusion, bf16[1,1,512,3,256]{2,4,3,1,0:T(8,128)(2,1)S(1)} %copy.130), kind=kOutput, calls=%fused_computation.14 | convolution fusion | flops 855638016 | bytes 5521408 | tf_op jit(solution)/shard_map/dot_general | solution.py:130
  178.3 7.6 %fusion.27 = bf16[1,1,4,8,32,256]{5,4,3,2,1,0:T(8,128)(2,1)} fusion(f32[4,8,34,3,256]{4,2,1,0,3:T(8,128)S(1)} %fusion.21, f32[4,8,34,3,256]{4,2,1,0,3:T(8,128)} %fusion.22, f32[4,8,34,3,256]{4,2,1,0,3:T(8,128)} %fusion.23, f32[4,8,34,3,256]{4,2,3,1,0:T(8,128)} %fusion.19, f32[4,8,34,3,256]{4,2,3,1,0:T(8,128)S(1)} %fusion.16, ...), kind=kLoop, calls=%fused_computation.35 | loop fusion | flops 7602176 | bytes 28836868 | tf_op jit(solution)/shard_map/convert_element_type | solution.py:135
  (59 shorter events, 4.5 us)
Async XLA Ops:
  16.9 14.6 %all-to-all-start = ((s32[8,1,192]{2,1,0:T(1,128)}), s32[8,1,192]{2,1,0:T(1,128)S(1)}, u32[]{:S(2)}, u32[]{:S(2)}) async-start(s32[8,1,192]{2,1,0:T(1,128)} %reshape.525), calls=%async_computation | async-start | bytes 16384 | tf_op jit(solution)/shard_map/all_to_all | solution.py:81
  30.2 47.0 %copy-start.9 = (s32[4]{0:T(128)S(1)}, s32[4]{0:T(128)}, u32[]{:S(2)}) copy-start(s32[4]{0:T(128)} %param.11) | copy-start | bytes 52
  31.5 42.4 %all-to-all-start.2 = ((bf16[4,8,48,512]{3,2,0,1:T(8,128)(2,1)}), bf16[4,8,48,512]{3,2,0,1:T(8,128)(2,1)S(1)}, u32[]{:S(2)}, u32[]{:S(2)}) async-start(bf16[4,8,48,512]{3,2,0,1:T(8,128)(2,1)} %copy.91), calls=%async_computation.2 | async-start | bytes 3145728 | tf_op jit(solution)/shard_map/all_to_all | solution.py:74
  73.9 7.0 %all-to-all-start.1 = ((s32[4,1,384]{2,1,0:T(1,128)}), s32[4,1,384]{2,1,0:T(1,128)S(1)}, u32[]{:S(2)}, u32[]{:S(2)}) async-start(s32[4,1,384]{2,1,0:T(1,128)} %reshape.527), calls=%async_computation.1 | async-start | bytes 12288 | tf_op jit(solution)/shard_map/all_to_all | solution.py:80
  81.0 28.7 %all-to-all-start.3 = ((bf16[4,8,48,512]{3,2,1,0:T(8,128)(2,1)}), bf16[4,8,48,512]{3,2,1,0:T(8,128)(2,1)}, u32[]{:S(2)}, u32[]{:S(2)}) async-start(bf16[4,8,48,512]{3,2,1,0:T(8,128)(2,1)} %copy.92), calls=%async_computation.3 | async-start | bytes 3145728 | tf_op jit(solution)/shard_map/all_to_all | solution.py:73
  109.7 45.9 %copy-start.6 = (f32[512]{0:T(512)S(1)}, f32[512]{0:T(512)}, u32[]{:S(2)}) copy-start(f32[512]{0:T(512)} %param.13) | copy-start | bytes 6148
  109.7 45.9 %copy-start.7 = (f32[512]{0:T(512)S(1)}, f32[512]{0:T(512)}, u32[]{:S(2)}) copy-start(f32[512]{0:T(512)} %param.12) | copy-start | bytes 6148
  118.7 26.0 %collective-permute-start = (bf16[4,8,1,512]{3,2,1,0:T(2,128)(2,1)S(1)}, bf16[4,8,1,512]{3,2,1,0:T(2,128)(2,1)S(1)}, u32[]{:S(2)}, u32[]{:S(2)}) collective-permute-start(bf16[4,8,1,512]{3,2,1,0:T(2,128)(2,1)S(1)} %get-tuple-element.20), channel_id=1, source_target_pairs={{0,4},{4,8},{8,12},{12,16},{16,20},{20,24},{24,28},{1,5},{5,9},{9,... | collective-permute-start | bytes 98312 | tf_op jit(solution)/shard_map/ppermute | solution.py:20
  122.7 22.1 %collective-permute-start.1 = (bf16[4,8,1,512]{3,2,1,0:T(2,128)(2,1)S(1)}, bf16[4,8,1,512]{3,2,1,0:T(2,128)(2,1)S(1)}, u32[]{:S(2)}, u32[]{:S(2)}) collective-permute-start(bf16[4,8,1,512]{3,2,1,0:T(2,128)(2,1)S(1)} %get-tuple-element.21), channel_id=1, source_target_pairs={{4,0},{8,4},{12,8},{16,12},{20,16},{24,20},{28,24},{5,1},{9,5},{13... | collective-permute-start | bytes 98312 | tf_op jit(solution)/shard_map/ppermute | solution.py:20
  145.0 4.2 %collective-permute-start.2 = (bf16[4,1,34,512]{3,2,1,0:T(8,128)(2,1)S(1)}, bf16[4,1,34,512]{3,2,1,0:T(8,128)(2,1)S(1)}, u32[]{:S(2)}, u32[]{:S(2)}) collective-permute-start(bf16[4,1,34,512]{3,2,1,0:T(8,128)(2,1)S(1)} %get-tuple-element.18), channel_id=1, source_target_pairs={{0,16},{4,20},{8,24},{12,28},{1,17},{5,21},{9,25},{13,29},{2,18},{... | collective-permute-start | bytes 417800 | tf_op jit(solution)/shard_map/ppermute | solution.py:20
  146.3 9.2 %collective-permute-start.3 = (bf16[4,1,34,512]{3,2,1,0:T(8,128)(2,1)S(1)}, bf16[4,1,34,512]{3,2,1,0:T(8,128)(2,1)S(1)}, u32[]{:S(2)}, u32[]{:S(2)}) collective-permute-start(bf16[4,1,34,512]{3,2,1,0:T(8,128)(2,1)S(1)} %get-tuple-element.19), channel_id=1, source_target_pairs={{16,0},{20,4},{24,8},{28,12},{17,1},{21,5},{25,9},{29,13},{18,2},{... | collective-permute-start | bytes 417800 | tf_op jit(solution)/shard_map/ppermute | solution.py:20
  158.0 2.5 %copy-start.3 = (bf16[1,1,512,3,256]{2,4,3,1,0:T(8,128)(2,1)S(1)}, bf16[1,1,512,3,256]{2,4,3,1,0:T(8,128)(2,1)}, u32[]{:S(2)}) copy-start(bf16[1,1,512,3,256]{2,4,3,1,0:T(8,128)(2,1)} %copy.131) | copy-start | bytes 2359300
  160.5 1.3 copy-start.2
  163.0 1.3 copy-start.1
  164.3 1.3 copy-start
  165.6 3.2 %copy-start.5 = (bf16[1,1,512,3,256]{2,4,3,1,0:T(8,128)(2,1)S(1)}, bf16[1,1,512,3,256]{2,4,3,1,0:T(8,128)(2,1)}, u32[]{:S(2)}) copy-start(bf16[1,1,512,3,256]{2,4,3,1,0:T(8,128)(2,1)} %copy.137) | copy-start | bytes 2359300
  168.7 3.2 %copy-start.4 = (bf16[1,1,512,3,256]{2,4,3,1,0:T(8,128)(2,1)S(1)}, bf16[1,1,512,3,256]{2,4,3,1,0:T(8,128)(2,1)}, u32[]{:S(2)}) copy-start(bf16[1,1,512,3,256]{2,4,3,1,0:T(8,128)(2,1)} %copy.138) | copy-start | bytes 2359300
  175.1 3.2 %copy-start.8 = (f32[256]{0:T(256)S(1)}, f32[256]{0:T(256)}, u32[]{:S(2)}) copy-start(f32[256]{0:T(256)} %param.15) | copy-start | bytes 3076
where the time goes:
time: 187 us; the launch traced here: 186 us
  local copies, waits for them, and re-layouts  47 us (25%)
  waiting for transfers between devices  43.4 us (23%)
  starting transfers between devices  28.1 us (15%)
  other arithmetic  24.4 us (13%)
  matrix products  21.3 us (11%)
  blocking collectives  20.7 us (11%)
    all_to_all x1, waiting for transfers between devices, on_device(): lax.all_to_all(outgoing, 'tile', split_axis=1, concat_axis=1, tiled=True)  34.5 us
    psum x1, blocking collectives, on_device(): first_sum, second_sum = lax.psum((first_sum, second_sum), 'tile')  20.7 us
    dot_general x9, matrix products, on_device(): product = jnp.dot(slab_rows, kernel, preferred_element_type=jnp.float32)  20.2 us
    unnamed x33, local copies, waits for them, and re-layouts  18.3 us
    another operation x2, other arithmetic  9.04 us
    scatter x1, local copies, waits for them, and re-layouts, on_device(): tile_rows = jnp.zeros((row_count, channels), jnp.bfloat16).at[arrived_slo...  8 us
    ppermute x4, waiting for transfers between devices, shifted(): return lax.ppermute(block, axis, route)  7.63 us
    convert_element_type x1, other arithmetic, on_device(): return decoded.astype(jnp.bfloat16)[None, None]  7.58 us
  transfers between devices with their start and end apart: 8, of which 4 were waited for; matrix products, arithmetic and copies ran while one was open for 20% of the time, Pallas kernels for 0%

commit v1 on v0

v1 whole, which is shorter than its diff:
```python
import functools

import jax
import jax.numpy as jnp
from jax import lax
from jax.experimental import pallas as pl
from jax.experimental.pallas import tpu as pltpu
from jax.sharding import PartitionSpec as P

GROUPS = 32
LT = 4
TH = 8
TW = 32
GW = 4
PLANE = TH * TW
LANES = 128
STAT = 64
EPSILON = 1e-06
HIGHEST = lax.Precision.HIGHEST
F32 = jnp.float32
BF16 = jnp.bfloat16
NT = (((1,), (1,)), ((), ()))
MESH = pl.DeviceIdType.MESH
EDGES = ((0, 1), (0, -1), (1, 0), (-1, 0), (1, 1), (1, -1), (-1, 1), (-1, -1))


def iota(shape, axis):
    return lax.broadcasted_iota(jnp.int32, shape, axis)


def bits(n):
    return n.bit_length() - 1


def dot(a, b, **kw):
    return jnp.dot(a, b, preferred_element_type=F32, **kw)


def route_kernel(
    tiles,
    clips,
    cap,
    live_ref,
    owner_ref,
    slot_ref,
    rows_ref,
    x_ref,
    cols_ref,
    faces_ref,
    corners_ref,
    stats_ref,
    send_rows,
    recv_rows,
    send_meta,
    recv_meta,
    total,
    edge_out,
    face_out,
    edge_in,
    face_in,
    row_sent,
    row_got,
    meta_sent,
    meta_got,
    halo_sent,
    halo_got,
):
    count = tiles * clips
    half = tiles // 2
    own = count // 2
    rows, channels = rows_ref.shape
    my_tile = lax.axis_index("tile")
    my_clip = lax.axis_index("clip")
    my_half = my_tile // half
    my_local = my_tile % half

    def partner(k):
        rest = k % own
        to_half = (my_half + 1 + k // own) % 2
        to_tile = to_half * half + (my_local + rest // clips) % half
        return to_tile, (my_clip + rest % clips) % clips

    for buffer in (edge_in, face_in):
        buffer[...] = jnp.zeros_like(buffer)
    barrier = pltpu.get_barrier_semaphore()

    @pl.loop(0, count)
    def _(k):
        @pl.when(k != own)
        def _():
            pl.semaphore_signal(barrier, inc=1, device_id=partner(k), device_id_type=MESH)

    owner = owner_ref[...]
    slot = slot_ref[...]
    table = (iota((count, rows), 0) == owner).astype(F32)
    before = (iota((rows, rows), 0) < iota((rows, rows), 1)).astype(F32).astype(BF16)
    rank = jnp.sum(dot(table.astype(BF16), before) * table, axis=0, keepdims=True)
    to_clip = owner >> bits(tiles)
    to_tile = owner & (tiles - 1)
    same = ((to_tile >> bits(half)) == my_half).astype(jnp.int32)
    turn = ((to_tile & (half - 1)) - my_local) & (half - 1)
    order = same * own + turn * clips + ((to_clip - my_clip) & (clips - 1))
    position = order * cap + rank.astype(jnp.int32)

    clip_row = iota((8, rows), 0)
    live_limit = jnp.zeros((8, rows), jnp.int32)
    for c in range(clips):
        live_limit = jnp.where(clip_row == c, live_ref[c] * PLANE, live_limit)
    mask = ((clip_row == to_clip) & (slot < live_limit)).astype(F32).astype(BF16)
    values = rows_ref[...]
    wide = values.astype(F32)
    square = wide * wide
    high = square.astype(BF16)
    low = (square - high.astype(F32)).astype(BF16)
    sum1 = dot(mask, values)
    sum2 = dot(mask, high) + dot(mask, low)
    per_group = bits(channels // GROUPS)
    group = iota((channels, LANES), 0) >> per_group
    lane = iota((channels, LANES), 1)
    partial = dot(sum1, (lane - STAT == group).astype(F32), precision=HIGHEST) + dot(
        sum2, (lane - STAT - GROUPS == group).astype(F32), precision=HIGHEST
    )

    digits_row = iota((8, rows), 0)
    digits = jnp.where(digits_row == 0, slot >> 5, jnp.where(digits_row == 1, slot & 31, 0))
    digits = digits.astype(F32).astype(BF16)

    batch = max(8, min(count, 512 // cap // 8 * 8))
    size = batch * cap
    segment = iota((batch, size), 0) * cap
    column = iota((batch, size), 1)
    inside = (column >= segment) & (column < segment + cap)
    piece = (iota((cap, LANES), 0) == iota((cap, LANES), 1)).astype(F32).astype(BF16)
    place = jnp.concatenate([piece] * batch, axis=0)
    goes = (my_clip + iota((batch, LANES), 0)) & (clips - 1)
    stats = jnp.zeros((batch, LANES), F32)
    for c in range(clips):
        stats = jnp.where(goes == c, partial[c : c + 1], stats)

    def row_copy(k):
        return pltpu.make_async_remote_copy(
            src_ref=send_rows.at[k],
            dst_ref=recv_rows.at[k],
            send_sem=row_sent.at[k],
            recv_sem=row_got.at[k],
            device_id=partner(k),
            device_id_type=MESH,
        )

    def meta_copy(k):
        return pltpu.make_async_remote_copy(
            src_ref=send_meta.at[k],
            dst_ref=recv_meta.at[k],
            send_sem=meta_sent.at[k],
            recv_sem=meta_got.at[k],
            device_id=partner(k),
            device_id_type=MESH,
        )

    for step in range(count // batch):
        first = step * batch
        chosen = (iota((size, rows), 0) + first * cap == position).astype(F32).astype(BF16)
        packed = dot(chosen, values).astype(BF16)
        send_rows[first : first + batch] = packed.reshape(batch, cap, channels)
        slots = lax.dot_general(digits, chosen, NT, preferred_element_type=F32)
        upper = jnp.where(inside, slots[0:1], 0.0).astype(BF16)
        lower = jnp.where(inside, slots[1:2], 0.0).astype(BF16)
        meta = dot(upper, place) * 32.0 + dot(lower, place) + stats
        for i in range(batch):
            send_meta[first + i] = meta[i : i + 1]
        if first <= own < first + batch:
            recv_rows[own] = send_rows[own]
            recv_meta[own] = send_meta[own]
        if step == 0:
            pl.semaphore_wait(barrier, count - 1)

        @pl.loop(first, first + batch)
        def _(k):
            @pl.when(k != own)
            def _():
                meta_copy(k).start()
                row_copy(k).start()

    joint = max(1, min(count, 256 // cap))
    while count % joint:
        joint -= 1
    width = joint * cap
    spread_lane = iota((LANES, width), 0)
    spread_col = iota((LANES, width), 1)
    spread = jnp.zeros((LANES, width), F32)
    owner_of = jnp.zeros((8, width), jnp.int32)
    for m in range(joint):
        hit = (spread_col - m * cap == spread_lane) & (spread_lane < cap)
        spread = jnp.where(hit, 1.0, spread)
        owner_of = jnp.where(iota((8, width), 1) >= m * cap, m, owner_of)
    voxel = iota((rows, width), 0)
    sums_in = jnp.zeros((1, LANES), F32)
    depth = (joint + 7) // 8
    for step in range(count // joint):
        first = step * joint

        @pl.loop(first, first + joint)
        def _(k):
            @pl.when(k != own)
            def _():
                meta_copy(k).wait_recv()
                row_copy(k).wait_recv()

        slot_row = jnp.zeros((1, width), F32)
        for d in range(depth):
            metas = jnp.zeros((8, LANES), F32)
            for m in range(d * 8, min(joint, d * 8 + 8)):
                one = recv_meta[first + m]
                sums_in = sums_in + one
                metas = jnp.where(iota((8, LANES), 0) == m - d * 8, one, metas)
            moved = dot(metas, spread, precision=HIGHEST)
            keep = owner_of == iota((8, width), 0) + d * 8
            slot_row = slot_row + jnp.sum(jnp.where(keep, moved, 0.0), axis=0, keepdims=True)
        target = (voxel == (slot_row + 0.5).astype(jnp.int32)).astype(F32).astype(BF16)
        arrived = recv_rows[first : first + joint].reshape(width, channels)
        placed = dot(target, arrived)
        if step == 0:
            total[...] = placed
        else:
            total[...] += placed
    stats_ref[...] = sums_in

    tile = total[...].astype(BF16)
    grid = tile.reshape(LT, TH, TW, channels)
    x_ref[...] = grid
    face_out[0] = grid[:, TH - 1].reshape(LT * TW, channels)
    face_out[1] = grid[:, 0].reshape(LT * TW, channels)
    line = iota((128, rows), 0)
    source = iota((128, rows), 1)
    wanted = jnp.where(
        line < 32,
        line * TW + TW - 1,
        jnp.where(line < 64, (line - 32) * TW, -1),
    )
    for e, (down, right) in enumerate(EDGES[4:]):
        base = 64 + e * 16
        offset = (TH - 1 if down > 0 else 0) * TW + (TW - 1 if right > 0 else 0)
        in_corner = (line >= base) & (line < base + LT)
        wanted = jnp.where(in_corner, (line - base) * PLANE + offset, wanted)
    edges = dot((source == wanted).astype(F32).astype(BF16), tile).astype(BF16)
    edge_out[...] = edges

    grid_rows = tiles // GW
    row_tile = my_tile // GW
    column_tile = my_tile % GW

    def exists(down, right):
        row = row_tile + down
        column = column_tile + right
        return (row >= 0) & (row < grid_rows) & (column >= 0) & (column < GW)

    def halo_copy(e):
        down, right = EDGES[e]
        if e < 2:
            part, source_ref, target_ref = pl.ds(e * 32, 32), edge_out, edge_in
        elif e < 4:
            part, source_ref, target_ref = e - 2, face_out, face_in
        else:
            part, source_ref, target_ref = pl.ds(64 + (e - 4) * 16, 16), edge_out, edge_in
        return pltpu.make_async_remote_copy(
            src_ref=source_ref.at[part],
            dst_ref=target_ref.at[part],
            send_sem=halo_sent.at[e],
            recv_sem=halo_got.at[e],
            device_id=(my_tile + down * GW + right, my_clip),
            device_id_type=MESH,
        )

    for e in (2, 3, 0, 1, 4, 5, 6, 7):
        @pl.when(exists(*EDGES[e]))
        def _():
            halo_copy(e).start()

    @pl.loop(0, count)
    def _(k):
        @pl.when(k != own)
        def _():
            meta_copy(k).wait_send()
            row_copy(k).wait_send()

    for e, (down, right) in enumerate(EDGES):
        @pl.when(exists(-down, -right))
        def _():
            halo_copy(e).wait_recv()

    cols_ref[...] = edge_in[0:64]
    corners_ref[...] = edge_in[64:128]
    faces_ref[...] = face_in[...]
    for e, (down, right) in enumerate(EDGES):
        @pl.when(exists(down, right))
        def _():
            halo_copy(e).wait_send()


def conv_kernel(
    tiles,
    info_ref,
    x_ref,
    cols_ref,
    faces_ref,
    corners_ref,
    stats_ref,
    gain_ref,
    bias_ref,
    out_bias_ref,
    weight_ref,
    out_ref,
    padded,
    summed,
    edge_act,
):
    tap = pl.program_id(0)
    channels = x_ref.shape[-1]
    live = info_ref[0]

    @pl.when(tap == 0)
    def _():
        per_group = channels // GROUPS
        voxels = jnp.full((8, LANES), live * (per_group * PLANE * tiles), jnp.int32)
        scaled = stats_ref[...] / voxels.astype(F32)
        lane = iota((LANES, channels), 0)
        group = iota((LANES, channels), 1) >> bits(per_group)
        mean = dot(scaled, (lane - STAT == group).astype(F32), precision=HIGHEST)
        second = dot(scaled, (lane - STAT - GROUPS == group).astype(F32), precision=HIGHEST)
        scale = lax.rsqrt(second - mean * mean + EPSILON)
        scale = (scale * gain_ref[...])[0:1]
        mean = mean[0:1]
        bias = bias_ref[...]

        def activate(raw):
            v = (raw.astype(F32) - mean) * scale + bias
            return v / (1.0 + jnp.exp(-v))

        up, down = info_ref[1] > 0, info_ref[2] > 0
        left, right = info_ref[3] > 0, info_ref[4] > 0
        zero = jnp.zeros((1, channels), F32)
        edge_act[0:32] = jnp.where(left, activate(cols_ref[0:32]), zero)
        edge_act[32:64] = jnp.where(right, activate(cols_ref[32:64]), zero)
        for e, ok in enumerate((up & left, up & right, down & left, down & right)):
            edge_act[64 + e * 16 : 80 + e * 16] = jnp.where(
                ok, activate(corners_ref[e * 16 : e * 16 + 16]), zero
            )
        where = iota((TW, channels), 0)

        def put(t, h, y, left_row, right_row):
            before = jnp.where(where == 0, left_row, pltpu.roll(y, 1, 0))
            after = jnp.where(where == TW - 1, right_row, pltpu.roll(y, TW - 1, 0))
            padded[t, h, :, 0:channels] = before.astype(BF16)
            padded[t, h, :, channels : 2 * channels] = y.astype(BF16)
            padded[t, h, :, 2 * channels : 3 * channels] = after.astype(BF16)

        @pl.loop(0, LT * TH)
        def _(r):
            t, h = r // TH, r % TH
            put(
                t,
                h + 1,
                activate(x_ref[t, h]),
                edge_act[pl.ds(r, 1)],
                edge_act[pl.ds(r + 32, 1)],
            )

        for side, ok in enumerate((up, down)):
            for t in range(LT):
                y = jnp.where(ok, activate(faces_ref[side, t * TW : (t + 1) * TW]), zero)
                base = 64 + side * 32 + t
                put(
                    t,
                    side * (TH + 1),
                    y,
                    edge_act[base : base + 1],
                    edge_act[base + 16 : base + 17],
                )
        summed[...] = jnp.zeros_like(summed)

    weight = weight_ref[0]
    for a in range(3):
        @pl.when(tap // 3 == a)
        def _():
            frames = LT - 2 + a
            slab = padded[0:frames, pl.ds(tap % 3, TH)].reshape(frames * PLANE, 3 * channels)
            start = (2 - a) * PLANE
            summed[start:, :] += dot(slab, weight)

    @pl.when(tap == 8)
    def _():
        frame = iota(summed.shape, 0) >> bits(PLANE)
        decoded = jnp.where(frame < live, summed[...] + out_bias_ref[...], 0.0)
        out_ref[...] = decoded.astype(BF16)


def on_device(
    seq_rows, plan_owner, plan_slot, live_frames, norm_gain, norm_bias, conv_weight, conv_bias
):
    rows, channels = seq_rows.shape
    out_width = conv_bias.shape[0]
    tiles = lax.axis_size("tile")
    clips = lax.axis_size("clip")
    count = tiles * clips
    cap = -(-(3 * (rows // count) // 2) // 16) * 16
    vmem = pl.BlockSpec(memory_space=pltpu.VMEM)
    smem = pl.BlockSpec(memory_space=pltpu.SMEM)
    dma = pltpu.SemaphoreType.DMA
    x, cols, faces, corners, stats = pl.pallas_call(
        functools.partial(route_kernel, tiles, clips, cap),
        out_shape=(
            jax.ShapeDtypeStruct((LT, TH, TW, channels), BF16),
            jax.ShapeDtypeStruct((64, channels), BF16),
            jax.ShapeDtypeStruct((2, LT * TW, channels), BF16),
            jax.ShapeDtypeStruct((64, channels), BF16),
            jax.ShapeDtypeStruct((1, LANES), F32),
        ),
        in_specs=[smem, vmem, vmem, vmem],
        out_specs=(vmem,) * 5,
        scratch_shapes=[
            pltpu.VMEM((count, cap, channels), BF16),
            pltpu.VMEM((count, cap, channels), BF16),
            pltpu.VMEM((count, 1, LANES), F32),
            pltpu.VMEM((count, 1, LANES), F32),
            pltpu.VMEM((rows, channels), F32),
            pltpu.VMEM((128, channels), BF16),
            pltpu.VMEM((2, LT * TW, channels), BF16),
            pltpu.VMEM((128, channels), BF16),
            pltpu.VMEM((2, LT * TW, channels), BF16),
            dma((count,)),
            dma((count,)),
            dma((count,)),
            dma((count,)),
            dma((8,)),
            dma((8,)),
        ],
        compiler_params=pltpu.CompilerParams(
            collective_id=0, has_side_effects=True, vmem_limit_bytes=48 << 20
        ),
        name="route",
    )(live_frames, plan_owner.reshape(1, rows), plan_slot.reshape(1, rows), seq_rows)

    my_tile = lax.axis_index("tile")
    row_tile, column_tile = my_tile // GW, my_tile % GW
    info = jnp.stack(
        [
            live_frames[lax.axis_index("clip")],
            (row_tile > 0).astype(jnp.int32),
            (row_tile < tiles // GW - 1).astype(jnp.int32),
            (column_tile > 0).astype(jnp.int32),
            (column_tile < GW - 1).astype(jnp.int32),
        ]
    )
    weight = conv_weight.transpose(0, 1, 3, 2, 4).reshape(9, 3 * channels, out_width)

    def whole(*shape):
        return pl.BlockSpec(shape, lambda i: (0,) * len(shape))

    decoded = pl.pallas_call(
        functools.partial(conv_kernel, tiles),
        grid=(9,),
        out_shape=jax.ShapeDtypeStruct((rows, out_width), BF16),
        in_specs=[
            smem,
            whole(LT, TH, TW, channels),
            whole(64, channels),
            whole(2, LT * TW, channels),
            whole(64, channels),
            whole(1, LANES),
            whole(1, channels),
            whole(1, channels),
            whole(1, out_width),
            pl.BlockSpec((1, 3 * channels, out_width), lambda i: (i, 0, 0)),
        ],
        out_specs=whole(rows, out_width),
        scratch_shapes=[
            pltpu.VMEM((LT, TH + 2, TW, 3 * channels), BF16),
            pltpu.VMEM((rows, out_width), F32),
            pltpu.VMEM((128, channels), F32),
        ],
        compiler_params=pltpu.CompilerParams(
            dimension_semantics=("arbitrary",), vmem_limit_bytes=32 << 20
        ),
        name="convolve",
    )(
        info,
        x,
        cols,
        faces,
        corners,
        stats,
        norm_gain.reshape(1, channels),
        norm_bias.reshape(1, channels),
        conv_bias.reshape(1, out_width),
        weight,
    )
    return decoded.reshape(1, 1, LT, TH, TW, out_width)


def solution(mesh):
    return jax.shard_map(
        on_device,
        mesh=mesh,
        in_specs=(
            P(("tile", "clip"), None),
            P(("tile", "clip")),
            P(("tile", "clip")),
            P(),
            P(),
            P(),
            P(),
            P(),
        ),
        out_specs=P("clip", "tile", None, None, None, None),
        check_vma=False,
    )
```

time: 187 us -> 79.3 us (0.42)
  the two profiles are of different devices: /device:TPU:0 before, /device:TPU:5 now
where the time goes in v1:
time: 79.3 us; the launch traced here: 78.9 us
  Pallas kernels  68.6 us (87%)
  local copies, waits for them, and re-layouts  10.3 us (13%)
    pallas_call x1, Pallas kernels, on_device(): pl.pallas_call(functools.partial(route_kernel, tiles, clips, cap), out_sh...  57 us
    pallas_call x1, Pallas kernels, on_device(): pl.pallas_call(functools.partial(conv_kernel, tiles), grid=(9,), out_shap...  11.6 us
    unnamed x16, local copies, waits for them, and re-layouts  8.3 us

profile of v1, /device:TPU:5, one launch (start us, length us, event | category | flops | bytes accessed | tf_op | source)
XLA Modules:
  0.0 78.9 jit_solution(5343818624971241643)
XLA Ops:
  0.0 1.2 %dynamic_slice.3 = s32[1]{0:T(128)} dynamic-slice(s32[4]{0:T(128)} %live_ref.1, s32[]{:T(128)S(6)} %select_n.14), dynamic_slice_sizes={1} | dynamic-slice | bytes 12 | tf_op jit(solution)/shard_map/dynamic_slice | solution.py:447
  1.2 0.7 stack.35.info_ref
  2.0 0.0 copy-start.1
  2.0 1.2 %copy-done.1 = bf16[1024,512]{1,0:T(8,128)(2,1)S(1)} copy-done((bf16[1024,512]{1,0:T(8,128)(2,1)S(1)}, bf16[1024,512]{1,0:T(8,128)(2,1)}, u32[]{:S(2)}) %copy-start.1) | copy-done | bytes 1048600
  3.2 0.0 copy-start.2
  3.2 0.7 copy-done.2
  3.9 0.0 copy-start.3
  3.9 0.7 copy-done.3
  4.6 0.0 copy-start.7
  4.6 0.7 copy-done.7
  5.2 57.0 %route.1 = (bf16[4,8,32,512]{3,2,1,0:T(8,128)(2,1)S(1)}, bf16[64,512]{1,0:T(8,128)(2,1)S(1)}, bf16[2,128,512]{2,1,0:T(8,128)(2,1)S(1)}, bf16[64,512]{1,0:T(8,128)(2,1)S(1)}, f32[1,128]{1,0:T(1,128)S(1)}) custom-call(s32[4]{0:T(128)S(1)} %copy-done.7, s32[1,1024]{1,0:T(1,128)S(1)} %bitcast.14, s32[1,1024]{1,0:T(1,128)S(1)} %bitcast.15, ...), custom_call_target="tpu_custom_call" | custom-call | tf_op jit(solution)/shard_map/route/pallas_call | solution.py:409
  62.3 0.0 copy-start
  62.3 3.0 %copy-done = bf16[3,3,512,3,256]{4,2,3,1,0:T(8,128)(2,1)S(1)} copy-done((bf16[3,3,512,3,256]{4,2,3,1,0:T(8,128)(2,1)S(1)}, bf16[3,3,512,3,256]{4,2,3,1,0:T(8,128)(2,1)}, u32[]{:S(2)}) %copy-start) | copy-done | bytes 7077912
  65.3 0.0 copy-start.4
  65.3 0.7 copy-done.4
  66.0 0.0 copy-start.5
  66.0 0.7 copy-done.5
  66.6 0.0 copy-start.6
  66.6 0.7 copy-done.6
  67.3 11.6 %convolve.1 = bf16[1024,256]{1,0:T(8,128)(2,1)} custom-call(s32[5]{0:T(128)S(1)} %stack.35.info_ref, bf16[4,8,32,512]{3,2,1,0:T(8,128)(2,1)S(1)} %get-tuple-element.10.x_ref, bf16[64,512]{1,0:T(8,128)(2,1)S(1)} %get-tuple-element.11.cols_ref, bf16[2,128,512]{2,1,0:T(8,128)(2,1)S(1)} %get-tuple-element.12.faces_ref, ...), custom_call_target="tpu_custom_call" | custom-call | tf_op jit(solution)/shard_map/convolve/pallas_call | solution.py:459
Async XLA Ops:
  2.0 1.2 %copy-start.1 = (bf16[1024,512]{1,0:T(8,128)(2,1)S(1)}, bf16[1024,512]{1,0:T(8,128)(2,1)}, u32[]{:S(2)}) copy-start(bf16[1024,512]{1,0:T(8,128)(2,1)} %rows_ref.1) | copy-start | bytes 3145732
  3.2 0.7 copy-start.2
  3.9 0.7 copy-start.3
  4.6 0.7 copy-start.7
  62.3 3.0 %copy-start = (bf16[3,3,512,3,256]{4,2,3,1,0:T(8,128)(2,1)S(1)}, bf16[3,3,512,3,256]{4,2,3,1,0:T(8,128)(2,1)}, u32[]{:S(2)}) copy-start(bf16[3,3,512,3,256]{4,2,3,1,0:T(8,128)(2,1)} %param.14) | copy-start | bytes 21233668
  65.3 0.7 copy-start.4
  66.0 0.7 copy-start.5
  66.6 0.7 copy-start.6

commit v2 on v1

--- a/solution.py
+++ b/solution.py
@@ -36,19 +36,27 @@
     return jnp.dot(a, b, preferred_element_type=F32, **kw)
 
 
-def route_kernel(
+def decode_kernel(
     tiles,
     clips,
     cap,
+    live_hbm,
+    owner_hbm,
+    slot_hbm,
+    rows_hbm,
+    gain_hbm,
+    bias_hbm,
+    out_bias_hbm,
+    weight_hbm,
+    out_ref,
     live_ref,
     owner_ref,
     slot_ref,
     rows_ref,
-    x_ref,
-    cols_ref,
-    faces_ref,
-    corners_ref,
-    stats_ref,
+    gain_ref,
+    bias_ref,
+    out_bias_ref,
+    weight_ref,
     send_rows,
     recv_rows,
     send_meta,
@@ -58,6 +66,10 @@
     face_out,
     edge_in,
     face_in,
+    padded,
+    summed,
+    edge_act,
+    loaded,
     row_sent,
     row_got,
     meta_sent,
@@ -65,9 +77,26 @@
     halo_sent,
     halo_got,
 ):
+    loads = [
+        pltpu.make_async_copy(source, target, loaded.at[i])
+        for i, (source, target) in enumerate(
+            (
+                (owner_hbm, owner_ref),
+                (slot_hbm, slot_ref),
+                (live_hbm, live_ref),
+                (rows_hbm, rows_ref),
+                (gain_hbm, gain_ref),
+                (bias_hbm, bias_ref),
+                (out_bias_hbm, out_bias_ref),
+                (weight_hbm, weight_ref),
+            )
+        )
+    ]
+    for load in loads:
+        load.start()
     count = tiles * clips
     half = tiles // 2
-    own = count // 2
+    own = 1
     rows, channels = rows_ref.shape
     my_tile = lax.axis_index("tile")
     my_clip = lax.axis_index("clip")
@@ -75,8 +104,8 @@
     my_local = my_tile % half
 
     def partner(k):
-        rest = k % own
-        to_half = (my_half + 1 + k // own) % 2
+        rest = k // 2
+        to_half = (my_half + 1 + k % 2) % 2
         to_tile = to_half * half + (my_local + rest // clips) % half
         return to_tile, (my_clip + rest % clips) % clips
 
@@ -90,6 +119,8 @@
         def _():
             pl.semaphore_signal(barrier, inc=1, device_id=partner(k), device_id_type=MESH)
 
+    for load in loads[:4]:
+        load.wait()
     owner = owner_ref[...]
     slot = slot_ref[...]
     table = (iota((count, rows), 0) == owner).astype(F32)
@@ -99,7 +130,7 @@
     to_tile = owner & (tiles - 1)
     same = ((to_tile >> bits(half)) == my_half).astype(jnp.int32)
     turn = ((to_tile & (half - 1)) - my_local) & (half - 1)
-    order = same * own + turn * clips + ((to_clip - my_clip) & (clips - 1))
+    order = 2 * (turn * clips + ((to_clip - my_clip) & (clips - 1))) + same
     position = order * cap + rank.astype(jnp.int32)
 
     clip_row = iota((8, rows), 0)
@@ -125,14 +156,14 @@
     digits = jnp.where(digits_row == 0, slot >> 5, jnp.where(digits_row == 1, slot & 31, 0))
     digits = digits.astype(F32).astype(BF16)
 
-    batch = max(8, min(count, 512 // cap // 8 * 8))
+    batch = max(2 * clips, min(count, 512 // cap // 8 * 8))
     size = batch * cap
     segment = iota((batch, size), 0) * cap
     column = iota((batch, size), 1)
     inside = (column >= segment) & (column < segment + cap)
     piece = (iota((cap, LANES), 0) == iota((cap, LANES), 1)).astype(F32).astype(BF16)
     place = jnp.concatenate([piece] * batch, axis=0)
-    goes = (my_clip + iota((batch, LANES), 0)) & (clips - 1)
+    goes = (my_clip + (iota((batch, LANES), 0) >> 1)) & (clips - 1)
     stats = jnp.zeros((batch, LANES), F32)
     for c in range(clips):
         stats = jnp.where(goes == c, partial[c : c + 1], stats)
@@ -223,11 +254,9 @@
             total[...] = placed
         else:
             total[...] += placed
-    stats_ref[...] = sums_in
 
     tile = total[...].astype(BF16)
     grid = tile.reshape(LT, TH, TW, channels)
-    x_ref[...] = grid
     face_out[0] = grid[:, TH - 1].reshape(LT * TW, channels)
     face_out[1] = grid[:, 0].reshape(LT * TW, channels)
     line = iota((128, rows), 0)
@@ -276,6 +305,83 @@
         def _():
             halo_copy(e).start()
 
+    for load in loads[4:]:
+        load.wait()
+    live = live_ref[my_clip]
+    voxels = jnp.full((8, LANES), live * ((channels // GROUPS) * PLANE * tiles), jnp.int32)
+    scaled = sums_in / voxels.astype(F32)
+    stat_lane = iota((LANES, channels), 0)
+    stat_group = iota((LANES, channels), 1) >> per_group
+    mean = dot(scaled, (stat_lane - STAT == stat_group).astype(F32), precision=HIGHEST)
+    second = dot(scaled, (stat_lane - STAT - GROUPS == stat_group).astype(F32), precision=HIGHEST)
+    scale = lax.rsqrt(second - mean * mean + EPSILON)
+    scale = (scale * gain_ref[...])[0:1]
+    mean = mean[0:1]
+    bias = bias_ref[...]
+
+    def activate(raw):
+        v = (raw.astype(F32) - mean) * scale + bias
+        u = 0.5 * v
+        return u + u * jnp.tanh(u)
+
+    for t in range(LT):
+        @pl.loop(0, TH, unroll=2)
+        def _(h):
+            y = activate(total[pl.ds(pl.multiple_of((t * TH + h) * TW, TW), TW)])
+            padded[t, h + 1, :, 0:channels] = pltpu.roll(y, 1, 0).astype(BF16)
+            padded[t, h + 1, :, channels : 2 * channels] = y.astype(BF16)
+            padded[t, h + 1, :, 2 * channels : 3 * channels] = pltpu.roll(y, TW - 1, 0).astype(BF16)
+
+    for e, (down, right) in enumerate(EDGES):
+        @pl.when(exists(-down, -right))
+        def _():
+            halo_copy(e).wait_recv()
+
+    zero = jnp.zeros((1, channels), F32)
+    for e, (down, right) in enumerate(EDGES):
+        if 2 <= e < 4:
+            continue
+        begin, end = (e * 32, e * 32 + 32) if e < 2 else (e * 16, e * 16 + 16)
+        edge_act[begin:end] = jnp.where(exists(-down, -right), activate(edge_in[begin:end]), zero)
+
+    where = iota((TW, channels), 0)
+    place16 = iota((16, channels), 0)
+
+    @pl.loop(0, LT * TH)
+    def _(r):
+        t, h = r // TH, r % TH + 1
+        head = padded[t, h, 0:16, 0:channels].astype(F32)
+        head = jnp.where(place16 == 0, edge_act[pl.ds(r, 1)], head)
+        padded[t, h, 0:16, 0:channels] = head.astype(BF16)
+        last = padded[t, h, TW - 16 : TW, 2 * channels : 3 * channels].astype(F32)
+        last = jnp.where(place16 == 15, edge_act[pl.ds(r + 32, 1)], last)
+        padded[t, h, TW - 16 : TW, 2 * channels : 3 * channels] = last.astype(BF16)
+
+    for side in range(2):
+        ok = exists(2 * side - 1, 0)
+        for t in range(LT):
+            y = jnp.where(ok, activate(face_in[side, t * TW : (t + 1) * TW]), zero)
+            base = 64 + side * 32 + t
+            before_y = jnp.where(where == 0, edge_act[base : base + 1], pltpu.roll(y, 1, 0))
+            after_y = jnp.where(
+                where == TW - 1, edge_act[base + 16 : base + 17], pltpu.roll(y, TW - 1, 0)
+            )
+            h = side * (TH + 1)
+            padded[t, h, :, 0:channels] = before_y.astype(BF16)
+            padded[t, h, :, channels : 2 * channels] = y.astype(BF16)
+            padded[t, h, :, 2 * channels : 3 * channels] = after_y.astype(BF16)
+
+    summed[...] = jnp.broadcast_to(out_bias_ref[...], summed.shape)
+    for a in range(3):
+        @pl.loop(0, 3)
+        def _(b):
+            frames = LT - 2 + a
+            slab = padded[0:frames, pl.ds(b, TH)].reshape(frames * PLANE, 3 * channels)
+            summed[(2 - a) * PLANE :, :] += dot(slab, weight_ref[a * 3 + b])
+
+    frame = iota(summed.shape, 0) >> bits(PLANE)
+    out_ref[...] = jnp.where(frame < live, summed[...], 0.0).astype(BF16)
+
     @pl.loop(0, count)
     def _(k):
         @pl.when(k != own)
@@ -284,114 +390,9 @@
             row_copy(k).wait_send()
 
     for e, (down, right) in enumerate(EDGES):
-        @pl.when(exists(-down, -right))
-        def _():
-            halo_copy(e).wait_recv()
-
-    cols_ref[...] = edge_in[0:64]
-    corners_ref[...] = edge_in[64:128]
-    faces_ref[...] = face_in[...]
-    for e, (down, right) in enumerate(EDGES):
         @pl.when(exists(down, right))
         def _():
             halo_copy(e).wait_send()
-
-
-def conv_kernel(
-    tiles,
-    info_ref,
-    x_ref,
-    cols_ref,
-    faces_ref,
-    corners_ref,
-    stats_ref,
-    gain_ref,
-    bias_ref,
-    out_bias_ref,
-    weight_ref,
-    out_ref,
-    padded,
-    summed,
-    edge_act,
-):
-    tap = pl.program_id(0)
-    channels = x_ref.shape[-1]
-    live = info_ref[0]
-
-    @pl.when(tap == 0)
-    def _():
-        per_group = channels // GROUPS
-        voxels = jnp.full((8, LANES), live * (per_group * PLANE * tiles), jnp.int32)
-        scaled = stats_ref[...] / voxels.astype(F32)
-        lane = iota((LANES, channels), 0)
-        group = iota((LANES, channels), 1) >> bits(per_group)
-        mean = dot(scaled, (lane - STAT == group).astype(F32), precision=HIGHEST)
-        second = dot(scaled, (lane - STAT - GROUPS == group).astype(F32), precision=HIGHEST)
-        scale = lax.rsqrt(second - mean * mean + EPSILON)
-        scale = (scale * gain_ref[...])[0:1]
-        mean = mean[0:1]
-        bias = bias_ref[...]
-
-        def activate(raw):
-            v = (raw.astype(F32) - mean) * scale + bias
-            return v / (1.0 + jnp.exp(-v))
-
-        up, down = info_ref[1] > 0, info_ref[2] > 0
-        left, right = info_ref[3] > 0, info_ref[4] > 0
-        zero = jnp.zeros((1, channels), F32)
-        edge_act[0:32] = jnp.where(left, activate(cols_ref[0:32]), zero)
-        edge_act[32:64] = jnp.where(right, activate(cols_ref[32:64]), zero)
-        for e, ok in enumerate((up & left, up & right, down & left, down & right)):
-            edge_act[64 + e * 16 : 80 + e * 16] = jnp.where(
-                ok, activate(corners_ref[e * 16 : e * 16 + 16]), zero
-            )
-        where = iota((TW, channels), 0)
-
-        def put(t, h, y, left_row, right_row):
-            before = jnp.where(where == 0, left_row, pltpu.roll(y, 1, 0))
-            after = jnp.where(where == TW - 1, right_row, pltpu.roll(y, TW - 1, 0))
-            padded[t, h, :, 0:channels] = before.astype(BF16)
-            padded[t, h, :, channels : 2 * channels] = y.astype(BF16)
-            padded[t, h, :, 2 * channels : 3 * channels] = after.astype(BF16)
-
-        @pl.loop(0, LT * TH)
-        def _(r):
-            t, h = r // TH, r % TH
-            put(
-                t,
-                h + 1,
-                activate(x_ref[t, h]),
-                edge_act[pl.ds(r, 1)],
-                edge_act[pl.ds(r + 32, 1)],
-            )
-
-        for side, ok in enumerate((up, down)):
-            for t in range(LT):
-                y = jnp.where(ok, activate(faces_ref[side, t * TW : (t + 1) * TW]), zero)
-                base = 64 + side * 32 + t
-                put(
-                    t,
-                    side * (TH + 1),
-                    y,
-                    edge_act[base : base + 1],
-                    edge_act[base + 16 : base + 17],
-                )
-        summed[...] = jnp.zeros_like(summed)
-
-    weight = weight_ref[0]
-    for a in range(3):
-        @pl.when(tap // 3 == a)
-        def _():
-            frames = LT - 2 + a
-            slab = padded[0:frames, pl.ds(tap % 3, TH)].reshape(frames * PLANE, 3 * channels)
-            start = (2 - a) * PLANE
-            summed[start:, :] += dot(slab, weight)
-
-    @pl.when(tap == 8)
-    def _():
-        frame = iota(summed.shape, 0) >> bits(PLANE)
-        decoded = jnp.where(frame < live, summed[...] + out_bias_ref[...], 0.0)
-        out_ref[...] = decoded.astype(BF16)
 
 
 def on_device(
@@ -403,21 +404,21 @@
     clips = lax.axis_size("clip")
     count = tiles * clips
     cap = -(-(3 * (rows // count) // 2) // 16) * 16
-    vmem = pl.BlockSpec(memory_space=pltpu.VMEM)
-    smem = pl.BlockSpec(memory_space=pltpu.SMEM)
     dma = pltpu.SemaphoreType.DMA
-    x, cols, faces, corners, stats = pl.pallas_call(
-        functools.partial(route_kernel, tiles, clips, cap),
-        out_shape=(
-            jax.ShapeDtypeStruct((LT, TH, TW, channels), BF16),
-            jax.ShapeDtypeStruct((64, channels), BF16),
-            jax.ShapeDtypeStruct((2, LT * TW, channels), BF16),
-            jax.ShapeDtypeStruct((64, channels), BF16),
-            jax.ShapeDtypeStruct((1, LANES), F32),
-        ),
-        in_specs=[smem, vmem, vmem, vmem],
-        out_specs=(vmem,) * 5,
+    decoded = pl.pallas_call(
+        functools.partial(decode_kernel, tiles, clips, cap),
+        out_shape=jax.ShapeDtypeStruct((rows, out_width), BF16),
+        in_specs=[pl.BlockSpec(memory_space=pl.ANY)] * 8,
+        out_specs=pl.BlockSpec(memory_space=pltpu.VMEM),
         scratch_shapes=[
+            pltpu.SMEM((clips,), jnp.int32),
+            pltpu.VMEM((1, rows), jnp.int32),
+            pltpu.VMEM((1, rows), jnp.int32),
+            pltpu.VMEM((rows, channels), BF16),
+            pltpu.VMEM((1, channels), F32),
+            pltpu.VMEM((1, channels), F32),
+            pltpu.VMEM((1, out_width), F32),
+            pltpu.VMEM((9, 3 * channels, out_width), BF16),
             pltpu.VMEM((count, cap, channels), BF16),
             pltpu.VMEM((count, cap, channels), BF16),
             pltpu.VMEM((count, 1, LANES), F32),
@@ -427,6 +428,10 @@
             pltpu.VMEM((2, LT * TW, channels), BF16),
             pltpu.VMEM((128, channels), BF16),
             pltpu.VMEM((2, LT * TW, channels), BF16),
+            pltpu.VMEM((LT, TH + 2, TW, 3 * channels), BF16),
+            pltpu.VMEM((rows, out_width), F32),
+            pltpu.VMEM((128, channels), F32),
+            dma((8,)),
             dma((count,)),
             dma((count,)),
             dma((count,)),
@@ -435,64 +440,18 @@
             dma((8,)),
         ],
         compiler_params=pltpu.CompilerParams(
-            collective_id=0, has_side_effects=True, vmem_limit_bytes=48 << 20
+            collective_id=0, has_side_effects=True, vmem_limit_bytes=56 << 20
         ),
-        name="route",
-    )(live_frames, plan_owner.reshape(1, rows), plan_slot.reshape(1, rows), seq_rows)
-
-    my_tile = lax.axis_index("tile")
-    row_tile, column_tile = my_tile // GW, my_tile % GW
-    info = jnp.stack(
-        [
-            live_frames[lax.axis_index("clip")],
-            (row_tile > 0).astype(jnp.int32),
-            (row_tile < tiles // GW - 1).astype(jnp.int32),
-            (column_tile > 0).astype(jnp.int32),
-            (column_tile < GW - 1).astype(jnp.int32),
-        ]
-    )
-    weight = conv_weight.transpose(0, 1, 3, 2, 4).reshape(9, 3 * channels, out_width)
-
-    def whole(*shape):
-        return pl.BlockSpec(shape, lambda i: (0,) * len(shape))
-
-    decoded = pl.pallas_call(
-        functools.partial(conv_kernel, tiles),
-        grid=(9,),
-        out_shape=jax.ShapeDtypeStruct((rows, out_width), BF16),
-        in_specs=[
-            smem,
-            whole(LT, TH, TW, channels),
-            whole(64, channels),
-            whole(2, LT * TW, channels),
-            whole(64, channels),
-            whole(1, LANES),
-            whole(1, channels),
-            whole(1, channels),
-            whole(1, out_width),
-            pl.BlockSpec((1, 3 * channels, out_width), lambda i: (i, 0, 0)),
-        ],
-        out_specs=whole(rows, out_width),
-        scratch_shapes=[
-            pltpu.VMEM((LT, TH + 2, TW, 3 * channels), BF16),
-            pltpu.VMEM((rows, out_width), F32),
-            pltpu.VMEM((128, channels), F32),
-        ],
-        compiler_params=pltpu.CompilerParams(
-            dimension_semantics=("arbitrary",), vmem_limit_bytes=32 << 20
-        ),
-        name="convolve",
+        name="decode",
     )(
-        info,
-        x,
-        cols,
-        faces,
-        corners,
-        stats,
+        live_frames,
+        plan_owner.reshape(1, rows),
+        plan_slot.reshape(1, rows),
+        seq_rows,
         norm_gain.reshape(1, channels),
         norm_bias.reshape(1, channels),
         conv_bias.reshape(1, out_width),
-        weight,
+        conv_weight.transpose(0, 1, 3, 2, 4).reshape(9, 3 * channels, out_width),
     )
     return decoded.reshape(1, 1, LT, TH, TW, out_width)
 

time: 79.3 us -> 65.9 us (0.83)
  local copies, waits for them, and re-layouts: 10.3 us -> 1.87 us
  Pallas kernels: 68.6 us -> 63.1 us
    unnamed x16 -> x1, local copies, waits for them, and re-layouts: 8.3 us -> 1.87 us
    pallas_call x2 -> x1, Pallas kernels: 68.6 us -> 63.1 us  [on_device(): pl.pallas_call(functools.partial(decode_kernel, tiles, clips, cap), out_s...]
    dynamic_slice x1 -> x0, local copies, waits for them, and re-layouts: 1.24 us -> none  [on_device(): live_frames[lax.axis_index('clip')]]
where the time goes in v2:
time: 65.9 us; the launch traced here: 65 us
  Pallas kernels  63.1 us (96%)
  local copies, waits for them, and re-layouts  1.87 us (3%)
    pallas_call x1, Pallas kernels, on_device(): pl.pallas_call(functools.partial(decode_kernel, tiles, clips, cap), out_s...  63.1 us
    unnamed x1, local copies, waits for them, and re-layouts  1.87 us

profile of v2, /device:TPU:5, one launch (start us, length us, event | category | flops | bytes accessed | tf_op | source)
XLA Modules:
  0.0 65.0 jit_solution(14894244418107035875)
XLA Ops:
  0.0 63.1 %decode.1 = bf16[1024,256]{1,0:T(8,128)(2,1)} custom-call(s32[4]{0:T(128)} %live_hbm.1, s32[1,1024]{1,0:T(1,128)} %bitcast.11, s32[1,1024]{1,0:T(1,128)} %bitcast.12, bf16[1024,512]{1,0:T(8,128)(2,1)} %rows_hbm.1, f32[1,512]{1,0:T(1,128)} %bitcast.13, f32[1,512]{1,0:T(1,128)} %bitcast.14, f32[1,256]{1,0:T(1,128)} %bitcast.15, bf16[9,1536,256]{2,1,0:T(8,128)(2,1)} %bitcast.9), custom_call_target="tpu_custom_call" | custom-call | tf_op jit(solution)/shard_map/decode/pallas_call | solution.py:408
  63.1 1.9 %copy.10 = bf16[1,1,4,8,32,256]{5,4,3,2,1,0:T(8,128)(2,1)} copy(bf16[1,1,4,8,32,256]{5,4,3,2,1,0:T(8,128)(2,1)} %bitcast.10) | data formatting | bytes 1048576

commit v3 on v2

--- a/solution.py
+++ b/solution.py
@@ -92,7 +92,7 @@
             )
         )
     ]
-    for load in loads:
+    for load in loads[:-1]:
         load.start()
     count = tiles * clips
     half = tiles // 2
@@ -133,24 +133,8 @@
     order = 2 * (turn * clips + ((to_clip - my_clip) & (clips - 1))) + same
     position = order * cap + rank.astype(jnp.int32)
 
-    clip_row = iota((8, rows), 0)
-    live_limit = jnp.zeros((8, rows), jnp.int32)
-    for c in range(clips):
-        live_limit = jnp.where(clip_row == c, live_ref[c] * PLANE, live_limit)
-    mask = ((clip_row == to_clip) & (slot < live_limit)).astype(F32).astype(BF16)
     values = rows_ref[...]
-    wide = values.astype(F32)
-    square = wide * wide
-    high = square.astype(BF16)
-    low = (square - high.astype(F32)).astype(BF16)
-    sum1 = dot(mask, values)
-    sum2 = dot(mask, high) + dot(mask, low)
     per_group = bits(channels // GROUPS)
-    group = iota((channels, LANES), 0) >> per_group
-    lane = iota((channels, LANES), 1)
-    partial = dot(sum1, (lane - STAT == group).astype(F32), precision=HIGHEST) + dot(
-        sum2, (lane - STAT - GROUPS == group).astype(F32), precision=HIGHEST
-    )
 
     digits_row = iota((8, rows), 0)
     digits = jnp.where(digits_row == 0, slot >> 5, jnp.where(digits_row == 1, slot & 31, 0))
@@ -163,10 +147,6 @@
     inside = (column >= segment) & (column < segment + cap)
     piece = (iota((cap, LANES), 0) == iota((cap, LANES), 1)).astype(F32).astype(BF16)
     place = jnp.concatenate([piece] * batch, axis=0)
-    goes = (my_clip + (iota((batch, LANES), 0) >> 1)) & (clips - 1)
-    stats = jnp.zeros((batch, LANES), F32)
-    for c in range(clips):
-        stats = jnp.where(goes == c, partial[c : c + 1], stats)
 
     def row_copy(k):
         return pltpu.make_async_remote_copy(
@@ -188,11 +168,48 @@
             device_id_type=MESH,
         )
 
+    def partial_sums():
+        clip_row = iota((8, rows), 0)
+        live_limit = jnp.zeros((8, rows), jnp.int32)
+        for c in range(clips):
+            live_limit = jnp.where(clip_row == c, live_ref[c] * PLANE, live_limit)
+        mask = ((clip_row == to_clip) & (slot < live_limit)).astype(F32).astype(BF16)
+        wide = values.astype(F32)
+        square = wide * wide
+        high = square.astype(BF16)
+        low = (square - high.astype(F32)).astype(BF16)
+        sum1 = dot(mask, values)
+        sum2 = dot(mask, high) + dot(mask, low)
+        group = iota((channels, LANES), 0) >> per_group
+        lane = iota((channels, LANES), 1)
+        partial = dot(sum1, (lane - STAT == group).astype(F32), precision=HIGHEST) + dot(
+            sum2, (lane - STAT - GROUPS == group).astype(F32), precision=HIGHEST
+        )
+
+        goes = (my_clip + (iota((batch, LANES), 0) >> 1)) & (clips - 1)
+        stats = jnp.zeros((batch, LANES), F32)
+        for c in range(clips):
+            stats = jnp.where(goes == c, partial[c : c + 1], stats)
+        return stats
+
     for step in range(count // batch):
         first = step * batch
         chosen = (iota((size, rows), 0) + first * cap == position).astype(F32).astype(BF16)
         packed = dot(chosen, values).astype(BF16)
         send_rows[first : first + batch] = packed.reshape(batch, cap, channels)
+        if first <= own < first + batch:
+            recv_rows[own] = send_rows[own]
+        if step == 0:
+            pl.semaphore_wait(barrier, count - 1)
+
+        @pl.loop(first, first + batch)
+        def _(k):
+            @pl.when(k != own)
+            def _():
+                row_copy(k).start()
+
+        if step == 0:
+            stats = partial_sums()
         slots = lax.dot_general(digits, chosen, NT, preferred_element_type=F32)
         upper = jnp.where(inside, slots[0:1], 0.0).astype(BF16)
         lower = jnp.where(inside, slots[1:2], 0.0).astype(BF16)
@@ -200,17 +217,15 @@
         for i in range(batch):
             send_meta[first + i] = meta[i : i + 1]
         if first <= own < first + batch:
-            recv_rows[own] = send_rows[own]
             recv_meta[own] = send_meta[own]
-        if step == 0:
-            pl.semaphore_wait(barrier, count - 1)
 
         @pl.loop(first, first + batch)
         def _(k):
             @pl.when(k != own)
             def _():
                 meta_copy(k).start()
-                row_copy(k).start()
+
+    loads[-1].start()
 
     joint = max(1, min(count, 256 // cap))
     while count % joint:
@@ -300,7 +315,7 @@
             device_id_type=MESH,
         )
 
-    for e in (2, 3, 0, 1, 4, 5, 6, 7):
+    for e in (0, 1, 2, 3, 4, 5, 6, 7):
         @pl.when(exists(*EDGES[e]))
         def _():
             halo_copy(e).start()
@@ -332,19 +347,22 @@
             padded[t, h + 1, :, channels : 2 * channels] = y.astype(BF16)
             padded[t, h + 1, :, 2 * channels : 3 * channels] = pltpu.roll(y, TW - 1, 0).astype(BF16)
 
-    for e, (down, right) in enumerate(EDGES):
+    zero = jnp.zeros((1, channels), F32)
+
+    def receive(e):
+        down, right = EDGES[e]
+
         @pl.when(exists(-down, -right))
         def _():
             halo_copy(e).wait_recv()
 
-    zero = jnp.zeros((1, channels), F32)
-    for e, (down, right) in enumerate(EDGES):
         if 2 <= e < 4:
-            continue
+            return
         begin, end = (e * 32, e * 32 + 32) if e < 2 else (e * 16, e * 16 + 16)
         edge_act[begin:end] = jnp.where(exists(-down, -right), activate(edge_in[begin:end]), zero)
 
-    where = iota((TW, channels), 0)
+    receive(0)
+    receive(1)
     place16 = iota((16, channels), 0)
 
     @pl.loop(0, LT * TH)
@@ -357,6 +375,19 @@
         last = jnp.where(place16 == 15, edge_act[pl.ds(r + 32, 1)], last)
         padded[t, h, TW - 16 : TW, 2 * channels : 3 * channels] = last.astype(BF16)
 
+    summed[...] = jnp.broadcast_to(out_bias_ref[...], summed.shape)
+    width_in = 3 * channels
+    for a in range(3):
+        @pl.loop(0, 3)
+        def _(b):
+            frames = LT - 2 + a
+            slab = padded[0:frames, pl.ds(b + 1, TH - 2)]
+            product = dot(slab.reshape(frames * (TH - 2) * TW, width_in), weight_ref[a * 3 + b])
+            summed[2 - a :, 1 : TH - 1] += product.reshape(frames, TH - 2, TW, -1)
+
+    for e in range(2, 8):
+        receive(e)
+    where = iota((TW, channels), 0)
     for side in range(2):
         ok = exists(2 * side - 1, 0)
         for t in range(LT):
@@ -371,16 +402,19 @@
             padded[t, h, :, channels : 2 * channels] = y.astype(BF16)
             padded[t, h, :, 2 * channels : 3 * channels] = after_y.astype(BF16)
 
-    summed[...] = jnp.broadcast_to(out_bias_ref[...], summed.shape)
     for a in range(3):
         @pl.loop(0, 3)
         def _(b):
             frames = LT - 2 + a
-            slab = padded[0:frames, pl.ds(b, TH)].reshape(frames * PLANE, 3 * channels)
-            summed[(2 - a) * PLANE :, :] += dot(slab, weight_ref[a * 3 + b])
-
-    frame = iota(summed.shape, 0) >> bits(PLANE)
-    out_ref[...] = jnp.where(frame < live, summed[...], 0.0).astype(BF16)
+            slab = jnp.concatenate([padded[0:frames, b], padded[0:frames, b + TH - 1]], axis=0)
+            product = dot(slab.reshape(2 * frames * TW, width_in), weight_ref[a * 3 + b])
+            product = product.reshape(2 * frames, TW, -1)
+            summed[2 - a :, 0] += product[:frames]
+            summed[2 - a :, TH - 1] += product[frames:]
+
+    frame = iota(summed.shape, 0)
+    decoded = jnp.where(frame < live, summed[...], 0.0).astype(BF16)
+    out_ref[...] = decoded.reshape(out_ref.shape)
 
     @pl.loop(0, count)
     def _(k):
@@ -408,7 +442,7 @@
     decoded = pl.pallas_call(
         functools.partial(decode_kernel, tiles, clips, cap),
         out_shape=jax.ShapeDtypeStruct((rows, out_width), BF16),
-        in_specs=[pl.BlockSpec(memory_space=pl.ANY)] * 8,
+        in_specs=[pl.BlockSpec(memory_space=pltpu.HBM)] * 8,
         out_specs=pl.BlockSpec(memory_space=pltpu.VMEM),
         scratch_shapes=[
             pltpu.SMEM((clips,), jnp.int32),
@@ -429,7 +463,7 @@
             pltpu.VMEM((128, channels), BF16),
             pltpu.VMEM((2, LT * TW, channels), BF16),
             pltpu.VMEM((LT, TH + 2, TW, 3 * channels), BF16),
-            pltpu.VMEM((rows, out_width), F32),
+            pltpu.VMEM((LT, TH, TW, out_width), F32),
             pltpu.VMEM((128, channels), F32),
             dma((8,)),
             dma((count,)),

time: 65.9 us -> 63.2 us (0.959)
  Pallas kernels: 63.1 us -> 60.4 us
    pallas_call x1, Pallas kernels: 63.1 us -> 60.4 us  [on_device(): pl.pallas_call(functools.partial(decode_kernel, tiles, clips, cap), out_s...]
where the time goes in v3:
time: 63.2 us; the launch traced here: 62.2 us
  Pallas kernels  60.4 us (96%)
  local copies, waits for them, and re-layouts  1.87 us (3%)
    pallas_call x1, Pallas kernels, on_device(): pl.pallas_call(functools.partial(decode_kernel, tiles, clips, cap), out_s...  60.4 us
    unnamed x1, local copies, waits for them, and re-layouts  1.87 us

profile of v3, /device:TPU:5, one launch (start us, length us, event | category | flops | bytes accessed | tf_op | source)
XLA Modules:
  0.0 62.2 jit_solution(16639837956097767575)
XLA Ops:
  0.0 60.4 %decode.1 = bf16[1024,256]{1,0:T(8,128)(2,1)} custom-call(s32[4]{0:T(128)} %live_hbm.1, s32[1,1024]{1,0:T(1,128)} %bitcast.11, s32[1,1024]{1,0:T(1,128)} %bitcast.12, bf16[1024,512]{1,0:T(8,128)(2,1)} %rows_hbm.1, f32[1,512]{1,0:T(1,128)} %bitcast.13, f32[1,512]{1,0:T(1,128)} %bitcast.14, f32[1,256]{1,0:T(1,128)} %bitcast.15, bf16[9,1536,256]{2,1,0:T(8,128)(2,1)} %bitcast.9), custom_call_target="tpu_custom_call" | custom-call | tf_op jit(solution)/shard_map/decode/pallas_call | solution.py:442
  60.4 1.9 %copy.10 = bf16[1,1,4,8,32,256]{5,4,3,2,1,0:T(8,128)(2,1)} copy(bf16[1,1,4,8,32,256]{5,4,3,2,1,0:T(8,128)(2,1)} %bitcast.10) | data formatting | bytes 1048576

commit v4 on v3

--- a/solution.py
+++ b/solution.py
@@ -104,10 +104,10 @@
     my_local = my_tile % half
 
     def partner(k):
-        rest = k // 2
-        to_half = (my_half + 1 + k % 2) % 2
-        to_tile = to_half * half + (my_local + rest // clips) % half
-        return to_tile, (my_clip + rest % clips) % clips
+        rest = lax.div(k, 2)
+        to_half = lax.rem(my_half + 1 + lax.rem(k, 2), 2)
+        to_tile = to_half * half + lax.rem(my_local + lax.div(rest, clips), half)
+        return to_tile, lax.rem(my_clip + lax.rem(rest, clips), clips)
 
     for buffer in (edge_in, face_in):
         buffer[...] = jnp.zeros_like(buffer)
@@ -119,12 +119,12 @@
         def _():
             pl.semaphore_signal(barrier, inc=1, device_id=partner(k), device_id_type=MESH)
 
-    for load in loads[:4]:
+    before = (iota((rows, rows), 0) < iota((rows, rows), 1)).astype(F32).astype(BF16)
+    for load in loads[:2]:
         load.wait()
     owner = owner_ref[...]
     slot = slot_ref[...]
     table = (iota((count, rows), 0) == owner).astype(F32)
-    before = (iota((rows, rows), 0) < iota((rows, rows), 1)).astype(F32).astype(BF16)
     rank = jnp.sum(dot(table.astype(BF16), before) * table, axis=0, keepdims=True)
     to_clip = owner >> bits(tiles)
     to_tile = owner & (tiles - 1)
@@ -133,6 +133,8 @@
     order = 2 * (turn * clips + ((to_clip - my_clip) & (clips - 1))) + same
     position = order * cap + rank.astype(jnp.int32)
 
+    for load in loads[2:4]:
+        load.wait()
     values = rows_ref[...]
     per_group = bits(channels // GROUPS)
 

time: 63.2 us -> 62.9 us (level)
  no operation moved by 1% of the time
where the time goes in v4:
time: 62.9 us; the launch traced here: 62 us
  Pallas kernels  60.1 us (96%)
  local copies, waits for them, and re-layouts  1.87 us (3%)
    pallas_call x1, Pallas kernels, on_device(): pl.pallas_call(functools.partial(decode_kernel, tiles, clips, cap), out_s...  60.1 us
    unnamed x1, local copies, waits for them, and re-layouts  1.87 us

profile of v4, /device:TPU:5, one launch (start us, length us, event | category | flops | bytes accessed | tf_op | source)
XLA Modules:
  0.0 62.0 jit_solution(3077806607363819297)
XLA Ops:
  0.0 60.1 %decode.1 = bf16[1024,256]{1,0:T(8,128)(2,1)} custom-call(s32[4]{0:T(128)} %live_hbm.1, s32[1,1024]{1,0:T(1,128)} %bitcast.11, s32[1,1024]{1,0:T(1,128)} %bitcast.12, bf16[1024,512]{1,0:T(8,128)(2,1)} %rows_hbm.1, f32[1,512]{1,0:T(1,128)} %bitcast.13, f32[1,512]{1,0:T(1,128)} %bitcast.14, f32[1,256]{1,0:T(1,128)} %bitcast.15, bf16[9,1536,256]{2,1,0:T(8,128)(2,1)} %bitcast.9), custom_call_target="tpu_custom_call" | custom-call | tf_op jit(solution)/shard_map/decode/pallas_call | solution.py:444
  60.1 1.9 %copy.10 = bf16[1,1,4,8,32,256]{5,4,3,2,1,0:T(8,128)(2,1)} copy(bf16[1,1,4,8,32,256]{5,4,3,2,1,0:T(8,128)(2,1)} %bitcast.10) | data formatting | bytes 1048576
